TPU v7x, 32 devices: a whole 2x2x4 slice. The times are simulated.
32 devices in a mesh: groups: 2 (over y), edge: 4 (over z), trip: 2 (over x), sub: 2 (over core).
Axes of the slice: x: 2, y: 2, z: 4, core: 2. Of those that a mesh axis runs over, the one named last changes fastest.
Arguments:
- edge_feat: float32 [128, 128, 512], P(('groups', 'edge'), ('trip', 'sub')), parts along dimension 0, may hold values from -6 to 6
- edge_counts: int32 [128], P(('groups', 'edge')), parts along dimension 0, may hold values from 64 to 128
- reverse: int32 [128], P('groups'), parts along dimension 0, may hold values from 0 to 63, as said below
- patterns: int32 [8, 4, 64, 2], P(('groups', 'edge'), ('trip', 'sub')), parts along dimension 0, may hold values from 0 to 15
- trip_count: int32 [8, 4], P(('groups', 'edge'), ('trip', 'sub')), parts along dimension 0, may hold values from 16 to 64, as said below
- coef: float32 [8, 4, 64, 128, 128], P(('groups', 'edge'), ('trip', 'sub')), parts along dimension 0, may hold values from -0.1875 to 0.1875
- down_weight: float32 [3, 512, 256], replicated, may hold values from -0.25 to 0.25
- up_weight: float32 [3, 256, 512], replicated, may hold values from -0.375 to 0.375
- dense_weight: float32 [3, 512, 512], replicated, may hold values from -0.25 to 0.25
Outputs:
- edge_out: float32 [128, 128, 512], P(('groups', 'edge'), ('trip', 'sub')), parts along dimension 0
There are 2 independent parts, one for each index of `groups`. A program takes and returns all parts, laid end to end along the dimension named above; an argument that names none is the same for every part. Nothing has to cross between parts.
Inputs may be any that keep to these rules, and one draw needn't show every extreme that they name: reverse is an involution without fixed points; reverse[c] lies on another index of edge than c; from one index of edge at most 8 clusters have their reverse on one other index, and that many in every draw. `trip_count`: some device has all 64 slots live in every draw.
All inputs are finite; a program needn't handle non-finite values.
Results may differ from a plain program's by a relative error of at most 0.0003.
Values sent between devices are 32-bit elements; how exact they have to be, the bound alone decides.
A program may use at most 128 MiB of HBM per device.

v0:
```python
import functools

import jax
import jax.numpy as jnp
from jax import lax
from jax.experimental import pallas as pl
from jax.experimental.pallas import tpu as pltpu
from jax.sharding import PartitionSpec as P

INV_THREE = 1.0 / 3.0**0.5
INV_TWO = 1.0 / 2.0**0.5
F32, BF16 = jnp.float32, jnp.bfloat16
MESH = pl.DeviceIdType.MESH
CHUNK = 8


def split(x):
    hi = x.astype(BF16)
    return hi, (x - hi.astype(F32)).astype(BF16)


def dot(a, b):
    return jnp.dot(a, b, preferred_element_type=F32)


def mm3(x, w_hi, w_lo):
    rows = x.shape[0]
    hi, lo = split(x)
    both = dot(jnp.concatenate([hi, lo], axis=0), w_hi)
    return both[:rows] + both[rows:] + dot(hi, w_lo)


def kernel(dims, tab, feat_hbm, coef_hbm, down_hbm, up_hbm, dense_hbm, out, *scratch):
    nt, ns, ne, eb, r, cap, slots, layers, blk, ft, de = dims
    nk, ranks, half, wide = r // CHUNK, nt * ns, eb // 2, ft // 2
    zr, scratch = scratch[: 2 * nk], scratch[2 * nk :]
    (coef, down, up, dense, down_h, down_l, up_h, up_l, dense_h, dense_l, c3, x3, run, part, recv1, recv2, agg, zs, gath, mask,
     in_sem, agx_s, agp_s, agf_s, ag_r, r1_s, r1_r, r2_s, r2_r, z_s, z_r, z_free) = scratch
    o_perm, o_src, o_same = 0, slots, 2 * slots
    o_last, o_has = 3 * slots, 3 * slots + eb
    o_zsrc = o_has + eb
    o_zpos = o_zsrc + ne * cap
    o_count = o_zpos + eb
    a, b, e = lax.axis_index("trip"), lax.axis_index("sub"), lax.axis_index("edge")
    other = lax.rem(b + 1, ns)
    me = a * ns + b

    rest = pl.ds(1, layers - 1)
    loads = [
        pltpu.make_async_copy(s, d, in_sem.at[i])
        for i, (s, d) in enumerate(((feat_hbm, out), (down_hbm.at[rest], down.at[rest]), (coef_hbm, coef), (up_hbm, up), (dense_hbm, dense), (down_hbm.at[0], down.at[0])))
    ]
    loads[5].start()
    loads[0].start()

    barrier = pltpu.get_barrier_semaphore()
    for o in range(1, nt):
        pl.semaphore_signal(barrier, inc=1, device_id={"trip": lax.rem(a + o, nt)}, device_id_type=MESH)
    pl.semaphore_signal(barrier, inc=1, device_id={"sub": other}, device_id_type=MESH)
    for o in range(1, ne):
        pl.semaphore_signal(barrier, inc=1, device_id={"edge": lax.rem(e + o, ne)}, device_id_type=MESH)

    def rows(k):
        return pl.ds(k * CHUNK, CHUNK)

    def remote(src, dst, send, recv, where):
        return pltpu.make_async_remote_copy(
            src_ref=src, dst_ref=dst, send_sem=send, recv_sem=recv, device_id=where, device_id_type=MESH
        )

    def cols(h):
        return pl.ds(h * wide, wide)

    def gather_piece(rank, k, h):
        return gath.at[rank, pl.ds(h * half, half), rows(k), :]

    def ag_cross(k, h, o):
        g = gather_piece(me, k, h)
        return remote(g, g, agx_s.at[2 * k + h, o], ag_r.at[2 * k + h, me], {"trip": lax.rem(a + o, nt)})

    def ag_pair(k, h):
        g = gather_piece(me, k, h)
        return remote(g, g, agp_s.at[2 * k + h], ag_r.at[2 * k + h, me], {"sub": other})

    def ag_forward(k, h, o):
        rank = lax.rem(a + o, nt) * ns + b
        g = gather_piece(rank, k, h)
        return remote(g, g, agf_s.at[2 * k + h, o], ag_r.at[2 * k + h, rank], {"sub": other})

    def ag_arrive(k, h, rank):
        g = gather_piece(rank, k, h)
        remote(g, g, agp_s.at[2 * k + h], ag_r.at[2 * k + h, rank], {"sub": other}).wait_recv()

    def pass_on(k):
        for h in range(2):
            for o in range(1, nt):
                ag_arrive(k, h, lax.rem(a + o, nt) * ns + b)
                ag_forward(k, h, o).start()

    def rs_pair(k, h):
        return remote(
            part.at[other, :, :, rows(k), cols(h)],
            recv1.at[:, :, rows(k), cols(h)],
            r1_s.at[2 * k + h],
            r1_r.at[2 * k + h],
            {"sub": other},
        )

    def rs_cross(k, h, o):
        peer = lax.rem(a + o, nt)
        return remote(
            part.at[b, peer, :, rows(k), cols(h)],
            recv2.at[a, :, rows(k), cols(h)],
            r2_s.at[2 * k + h, o],
            r2_r.at[2 * k + h, a],
            {"trip": peer},
        )

    def rs_arrive(k, h, o):
        src = lax.rem(a + o, nt)
        dst = recv2.at[src, :, rows(k), cols(h)]
        remote(dst, dst, r2_s.at[2 * k + h, o], r2_r.at[2 * k + h, src], {"trip": src}).wait_recv()

    def z_copy(k, h, o):
        peer = lax.rem(e + o, ne)
        return remote(
            zs.at[pl.ds(peer * cap, cap), rows(k), cols(h)],
            zr[2 * k + h].at[pl.ds(e * cap, cap)],
            z_s.at[2 * k + h, o],
            z_r.at[2 * k + h, e],
            {"edge": peer},
        )

    def z_arrive(k, h, o):
        src = lax.rem(e + o, ne)
        dst = zr[2 * k + h].at[pl.ds(src * cap, cap)]
        remote(dst, dst, z_s.at[2 * k + h, o], z_r.at[2 * k + h, src], {"edge": src}).wait_recv()

    def lower(k, layer):
        for h in range(2):
            f = out[h * half : (h + 1) * half, rows(k), :].reshape(half * CHUNK, de)
            live = jnp.concatenate([mask[k, h * half * CHUNK : (h + 1) * half * CHUNK, :]] * (ft // 128), axis=1)
            low = mm3(f, down_h[layer], down_l[layer]) * live
            gath[me, h * half : (h + 1) * half, rows(k), :] = low.reshape(half, CHUNK, ft)
            for o in range(1, nt):
                ag_cross(k, h, o).start()
            ag_pair(k, h).start()

    for k in range(nk):
        ids = me * r + k * CHUNK + lax.broadcasted_iota(jnp.int32, (CHUNK, 128), 0)
        for c in range(eb):
            mask[k, c * CHUNK : (c + 1) * CHUNK, :] = jnp.where(ids < tab[o_count + c], 1.0, 0.0).astype(F32)
    loads[5].wait()
    loads[0].wait()
    for i in (2, 3, 4, 1):
        loads[i].start()

    def split_down(i, _):
        hi, lo = split(down[i])
        down_h[i] = hi
        down_l[i] = lo
        return 0

    split_down(0, 0)
    pl.semaphore_wait(barrier, nt - 1 + 1 + ne - 1)
    for k in range(nk):
        lower(k, 0)
    loads[2].wait()

    def split_coef(p, _):
        hi, lo = split(coef[tab[o_perm + p]])
        c3[p, :, 0:blk] = hi
        c3[p, :, blk : 2 * blk] = lo
        c3[p, :, 2 * blk : 3 * blk] = hi
        return 0

    lax.fori_loop(0, slots, split_coef, 0)
    for i in (3, 4, 1):
        loads[i].wait()
    lax.fori_loop(1, layers, split_down, 0)

    def split_rest(i, _):
        hi, lo = split(up[i])
        up_h[i] = hi
        up_l[i] = lo
        hi, lo = split(dense[i])
        dense_h[i] = hi
        dense_l[i] = lo
        return 0

    lax.fori_loop(0, layers, split_rest, 0)
    run[0] = jnp.zeros((blk, ft), F32)
    for k in range(nk - 2):
        pass_on(k)

    def layer_step(layer, _):
        if nk > 2:
            pass_on(nk - 2)

        def widen(first):
            def step(c, _):
                for rank in range(ranks):
                    hi, lo = split(gath[rank, c, first : first + 2 * CHUNK, :])
                    at = rank * r + first
                    x3[c, at : at + 2 * CHUNK, :] = hi
                    x3[c, blk + at : blk + at + 2 * CHUNK, :] = hi
                    x3[c, 2 * blk + at : 2 * blk + at + 2 * CHUNK, :] = lo
                return 0

            lax.fori_loop(0, eb, step, 0, unroll=4)

        for pair in range(nk // 2):
            if pair == nk // 2 - 1:
                for k in range(nk - 1 if nk > 2 else 0, nk):
                    pass_on(k)
            for k in (2 * pair, 2 * pair + 1):
                for h in range(2):
                    for o in range(nt):
                        ag_arrive(k, h, lax.rem(a + o, nt) * ns + other)
            widen(2 * pair * CHUNK)
        for k in range(nk):
            for h in range(2):
                ag_pair(k, h).wait_send()
                for o in range(1, nt):
                    ag_cross(k, h, o).wait_send()
                    ag_forward(k, h, o).wait_send()

        unroll = 16

        def triplets(i, _):
            for u in range(unroll):
                p = i * unroll + u
                keep = tab[o_same + p].astype(F32)
                run[p + 1] = run[p] * keep + dot(c3[p], x3[tab[o_src + p]])
            return 0

        lax.fori_loop(0, slots // unroll, triplets, 0)

        def cross(k):
            for h in range(2):
                rs_pair(k, h).wait_recv()
                for o in range(1, nt):
                    peer = lax.rem(a + o, nt)
                    part[b, peer, :, rows(k), cols(h)] = (
                        part[b, peer, :, rows(k), cols(h)] + recv1[peer, :, rows(k), cols(h)]
                    )
                    rs_cross(k, h, o).start()
                agg[:, rows(k), cols(h)] = part[b, a, :, rows(k), cols(h)] + recv1[a, :, rows(k), cols(h)]

        for k in range(nk):

            def collect(t, _):
                at, has = tab[o_last + t] + 1, tab[o_has + t].astype(F32)
                for rank in range(ranks):
                    first = rank * r + k * CHUNK
                    part[rank % ns, rank // ns, t, rows(k), :] = run[at, first : first + CHUNK, :] * has
                return 0

            lax.fori_loop(0, eb, collect, 0, unroll=4)
            for h in range(2):
                rs_pair(k, h).start()
            if k > 0:
                cross(k - 1)
        cross(nk - 1)

        @pl.when(layer > 0)
        def _():
            pl.semaphore_wait(z_free, ne - 1)

        for k in range(nk):
            for h in range(2):
                total = agg[:, rows(k), cols(h)]
                for o in range(1, nt):
                    rs_arrive(k, h, o)
                    total = total + recv2[lax.rem(a + o, nt), :, rows(k), cols(h)]
                agg[:, rows(k), cols(h)] = total
                for o in range(1, ne):
                    base = lax.rem(e + o, ne) * cap
                    for s in range(cap):
                        zs[base + s, rows(k), cols(h)] = agg[tab[o_zsrc + base + s], rows(k), cols(h)]
                    z_copy(k, h, o).start()
        for k in range(nk):
            sides = []
            for h in range(2):
                for o in range(1, ne):
                    z_arrive(k, h, o)
                sides.append(
                    jnp.concatenate(
                        [agg[c, rows(k), cols(h)] + zr[2 * k + h][tab[o_zpos + c]] for c in range(eb)], axis=0
                    )
                )
            both = jnp.concatenate(sides, axis=1)
            lifted = mm3(both, up_h[layer], up_l[layer])
            f = out[:, rows(k), :].reshape(eb * CHUNK, de)
            mixed = (f + lifted) * INV_THREE
            v = mm3(mixed, dense_h[layer], dense_l[layer])
            new = (mixed + v / (1.0 + jnp.exp(-v))) * jnp.where(layer + 1 < layers, INV_TWO, 1.0)
            out[:, rows(k), :] = new.reshape(eb, CHUNK, de)

            @pl.when(layer + 1 < layers)
            def _():
                lower(k, layer + 1)
                if k >= 2:
                    pass_on(k - 2)

        @pl.when(layer + 1 < layers)
        def _():
            for o in range(1, ne):
                pl.semaphore_signal(z_free, inc=1, device_id={"edge": lax.rem(e + o, ne)}, device_id_type=MESH)

        for k in range(nk):
            for h in range(2):
                rs_pair(k, h).wait_send()
                for o in range(1, nt):
                    rs_cross(k, h, o).wait_send()
                for o in range(1, ne):
                    z_copy(k, h, o).wait_send()
        return 0

    lax.fori_loop(0, layers, layer_step, 0)


def local(edge_feat, edge_counts, reverse, patterns, trip_count, coef, down_weight, up_weight, dense_weight):
    eb, r, de = edge_feat.shape
    nt, ns, ne = lax.axis_size("trip"), lax.axis_size("sub"), lax.axis_size("edge")
    layers, _, ft = down_weight.shape
    _, _, slots, blk, _ = coef.shape
    nk, ranks = r // CHUNK, nt * ns
    edge_rank = lax.axis_index("edge")
    cap = 2 * ((eb // 2 + ne // 2 - 1) // (ne // 2))
    i32 = jnp.int32
    ids = jnp.arange(slots, dtype=i32)
    key = jnp.where(ids < trip_count[0, 0], patterns[0, 0, :, 0], eb)
    before = (key[None, :] < key[:, None]) | ((key[None, :] == key[:, None]) & (ids[None, :] < ids[:, None]))
    rank = jnp.sum(before.astype(i32), axis=1)
    hot = (rank[None, :] == ids[:, None]).astype(i32)
    perm = jnp.sum(hot * ids[None, :], axis=1)
    source = jnp.sum(hot * patterns[0, 0, :, 1][None, :], axis=1)
    first = jnp.sum((key[None, :] < key[:, None]).astype(i32), axis=1)
    same = jnp.sum(hot * (first < rank).astype(i32)[None, :], axis=1)
    cl = jnp.arange(eb, dtype=i32)
    upto = jnp.sum((key[None, :] <= cl[:, None]).astype(i32), axis=1)
    has = jnp.any(key[None, :] == cl[:, None], axis=1).astype(i32)
    last = jnp.maximum(upto - 1, 0)
    mine = lax.dynamic_slice_in_dim(reverse, edge_rank * eb, eb)
    dev = mine // eb
    send_slot = jnp.sum(((dev[:, None] == dev[None, :]) & (cl[None, :] < cl[:, None])).astype(i32), axis=1)
    zslots = jnp.arange(ne * cap, dtype=i32)
    zsrc = jnp.sum(jnp.where(zslots[:, None] == (dev * cap + send_slot)[None, :], cl[None, :], 0), axis=1)
    all_ids = jnp.arange(reverse.shape[0], dtype=i32)
    match = (
        (all_ids[None, :] // eb == dev[:, None])
        & (all_ids[None, :] < mine[:, None])
        & (reverse[None, :] // eb == edge_rank)
    )
    zpos = dev * cap + jnp.sum(match.astype(i32), axis=1)
    tab = jnp.concatenate([perm, source, same, last, has, zsrc, zpos, edge_counts]).astype(i32)

    dims = (nt, ns, ne, eb, r, cap, slots, layers, blk, ft, de)
    vm = pltpu.VMEM
    dma = pltpu.SemaphoreType.DMA
    scratch = [vm((ne * cap, CHUNK, ft // 2), F32) for _ in range(2 * nk)] + [
        vm((slots, blk, blk), F32),
        vm(down_weight.shape, F32),
        vm(up_weight.shape, F32),
        vm(dense_weight.shape, F32),
        vm(down_weight.shape, BF16),
        vm(down_weight.shape, BF16),
        vm(up_weight.shape, BF16),
        vm(up_weight.shape, BF16),
        vm(dense_weight.shape, BF16),
        vm(dense_weight.shape, BF16),
        vm((slots, blk, 3 * blk), BF16),
        vm((eb, 3 * blk, ft), BF16),
        vm((slots + 1, blk, ft), F32),
        vm((ns, nt, eb, r, ft), F32),
        vm((nt, eb, r, ft), F32),
        vm((nt, eb, r, ft), F32),
        vm((eb, r, ft), F32),
        vm((ne * cap, r, ft), F32),
        vm((ranks, eb, r, ft), F32),
        vm((nk, eb * CHUNK, 128), F32),
        dma((6,)),
        dma((2 * nk, nt)),
        dma((2 * nk,)),
        dma((2 * nk, nt)),
        dma((2 * nk, ranks)),
        dma((2 * nk,)),
        dma((2 * nk,)),
        dma((2 * nk, nt)),
        dma((2 * nk, nt)),
        dma((2 * nk, ne)),
        dma((2 * nk, ne)),
        pltpu.SemaphoreType.REGULAR,
    ]
    anywhere = pl.BlockSpec(memory_space=pl.ANY)
    unscaled = pl.pallas_call(
        functools.partial(kernel, dims),
        out_shape=jax.ShapeDtypeStruct(edge_feat.shape, F32),
        in_specs=[pl.BlockSpec(memory_space=pltpu.SMEM)] + [anywhere] * 5,
        out_specs=pl.BlockSpec(memory_space=pltpu.VMEM),
        scratch_shapes=scratch,
        compiler_params=pltpu.CompilerParams(collective_id=0, has_side_effects=True, vmem_limit_bytes=64 * 1024 * 1024 - 65536),
    )(tab, edge_feat, coef[0, 0], down_weight, up_weight, dense_weight)
    return unscaled * INV_TWO


def solution(mesh):
    placed = (
        P(("groups", "edge"), ("trip", "sub"), None),
        P(("groups", "edge")),
        P("groups"),
        P(("groups", "edge"), ("trip", "sub"), None, None),
        P(("groups", "edge"), ("trip", "sub")),
        P(("groups", "edge"), ("trip", "sub"), None, None, None),
        P(),
        P(),
        P(),
    )
    return jax.shard_map(
        local,
        mesh=mesh,
        in_specs=placed,
        out_specs=P(("groups", "edge"), ("trip", "sub"), None),
        check_vma=False,
    )
```

profile of v0, /device:TPU:0, one launch (start us, length us, event | category | flops | bytes accessed | tf_op | source)
XLA Modules:
  0.0 138.1 jit_solution(17515728296418323688)
XLA Ops:
  0.7 0.7 compare_select_fusion
  1.3 0.7 fusion.6
  2.0 0.1 convert_reduce_fusion.3
  2.1 0.1 fusion.2
  2.2 0.7 slice_bitcast_fusion
  2.9 0.2 fusion
  3.1 0.1 select_reduce_fusion
  3.3 0.7 and_select_fusion.2
  4.0 0.2 convert_reduce_fusion.1
  4.2 0.2 convert_reduce_fusion.2
  4.4 0.1 select_reduce_fusion.3
  4.5 1.3 concatenate.3.tab
  5.8 130.0 %shard_map.91 = f32[16,32,512]{2,1,0:T(8,128)} custom-call(s32[288]{0:T(512)} %concatenate.3.tab, f32[16,32,512]{2,1,0:T(8,128)} %feat_hbm.1, f32[64,128,128]{2,1,0:T(8,128)} %bitcast.7, f32[3,512,256]{2,1,0:T(8,128)} %down_hbm.1, f32[3,256,512]{2,1,0:T(8,128)} %up_hbm.1, f32[3,512,512]{2,1,0:T(8,128)} %dense_hbm.1), custom_call_target="tpu_custom_call" | custom-call | tf_op jit(solution)/shard_map/pallas_call | solution.py:397
  135.8 2.3 %broadcast_multiply_fusion = f32[16,32,512]{2,1,0:T(8,128)} fusion(f32[16,32,512]{2,1,0:T(8,128)} %shard_map.91), kind=kLoop, calls=%fused_computation | loop fusion | flops 262144 | bytes 2097152 | tf_op jit(solution)/shard_map/mul | solution.py:405
  (4 shorter events, 0.0 us)
where the time goes:
time: 138 us
  Pallas kernels  130 us (94%)
  other arithmetic  5.44 us (4%)
  local copies, waits for them, and re-layouts  2.01 us (1%)
    pallas_call x1, Pallas kernels, local(): pl.pallas_call(functools.partial(kernel, dims), out_shape=jax.ShapeDtypeS...  130 us

commit v1 on v0

--- a/solution.py
+++ b/solution.py
@@ -32,10 +32,11 @@
 
 def kernel(dims, tab, feat_hbm, coef_hbm, down_hbm, up_hbm, dense_hbm, out, *scratch):
     nt, ns, ne, eb, r, cap, slots, layers, blk, ft, de = dims
-    nk, ranks, half, wide = r // CHUNK, nt * ns, eb // 2, ft // 2
+    nk, ranks, wide = r // CHUNK, nt * ns, ft // 2
+    early = nk - 2 if nk > 2 else 0
     zr, scratch = scratch[: 2 * nk], scratch[2 * nk :]
-    (coef, down, up, dense, down_h, down_l, up_h, up_l, dense_h, dense_l, c3, x3, run, part, recv1, recv2, agg, zs, gath, mask,
-     in_sem, agx_s, agp_s, agf_s, ag_r, r1_s, r1_r, r2_s, r2_r, z_s, z_r, z_free) = scratch
+    (coef, down, up, dense, down_h, down_l, up_h, up_l, dense_h, dense_l, c2, x2, run, part, recv1, recv2, agg, zs, gath, mask,
+     in_sem, agx_s, agy_s, agp_s, agf_s, ag_r, r1_s, r1_r, r2_s, r2_r, z_s, z_r, z_free) = scratch
     o_perm, o_src, o_same = 0, slots, 2 * slots
     o_last, o_has = 3 * slots, 3 * slots + eb
     o_zsrc = o_has + eb
@@ -55,35 +56,46 @@
 
     barrier = pltpu.get_barrier_semaphore()
     for o in range(1, nt):
-        pl.semaphore_signal(barrier, inc=1, device_id={"trip": lax.rem(a + o, nt)}, device_id_type=MESH)
+        for s in (b, other):
+            pl.semaphore_signal(barrier, inc=1, device_id={"trip": lax.rem(a + o, nt), "sub": s}, device_id_type=MESH)
     pl.semaphore_signal(barrier, inc=1, device_id={"sub": other}, device_id_type=MESH)
     for o in range(1, ne):
         pl.semaphore_signal(barrier, inc=1, device_id={"edge": lax.rem(e + o, ne)}, device_id_type=MESH)
 
     def rows(k):
         return pl.ds(k * CHUNK, CHUNK)
+
+    def cols(h):
+        return pl.ds(h * wide, wide)
 
     def remote(src, dst, send, recv, where):
         return pltpu.make_async_remote_copy(
             src_ref=src, dst_ref=dst, send_sem=send, recv_sem=recv, device_id=where, device_id_type=MESH
         )
 
-    def cols(h):
-        return pl.ds(h * wide, wide)
+    def trip(o):
+        return lax.rem(a + o, nt)
+
+    def both_cores(k, h):
+        return False
 
     def gather_piece(rank, k, h):
-        return gath.at[rank, pl.ds(h * half, half), rows(k), :]
-
-    def ag_cross(k, h, o):
+        return gath.at[rank, :, rows(k), cols(h)]
+
+    def ag_far(k, h, o):
         g = gather_piece(me, k, h)
-        return remote(g, g, agx_s.at[2 * k + h, o], ag_r.at[2 * k + h, me], {"trip": lax.rem(a + o, nt)})
+        return remote(g, g, agx_s.at[2 * k + h, o], ag_r.at[2 * k + h, me], {"trip": trip(o), "sub": other})
+
+    def ag_near(k, h, o):
+        g = gather_piece(me, k, h)
+        return remote(g, g, agy_s.at[2 * k + h, o], ag_r.at[2 * k + h, me], {"trip": trip(o), "sub": b})
 
     def ag_pair(k, h):
         g = gather_piece(me, k, h)
         return remote(g, g, agp_s.at[2 * k + h], ag_r.at[2 * k + h, me], {"sub": other})
 
     def ag_forward(k, h, o):
-        rank = lax.rem(a + o, nt) * ns + b
+        rank = trip(o) * ns + other
         g = gather_piece(rank, k, h)
         return remote(g, g, agf_s.at[2 * k + h, o], ag_r.at[2 * k + h, rank], {"sub": other})
 
@@ -91,15 +103,32 @@
         g = gather_piece(rank, k, h)
         remote(g, g, agp_s.at[2 * k + h], ag_r.at[2 * k + h, rank], {"sub": other}).wait_recv()
 
-    def pass_on(k):
-        for h in range(2):
+    def ag_send(k, h):
+        for o in range(1, nt):
+            ag_far(k, h, o).start()
+            if both_cores(k, h):
+                ag_near(k, h, o).start()
+        ag_pair(k, h).start()
+
+    def pass_on(k, h):
+        for o in range(1, nt):
+            ag_arrive(k, h, trip(o) * ns + other)
+            if not both_cores(k, h):
+                ag_forward(k, h, o).start()
+
+    def ag_finish(h):
+        for k in range(nk):
+            ag_pair(k, h).wait_send()
             for o in range(1, nt):
-                ag_arrive(k, h, lax.rem(a + o, nt) * ns + b)
-                ag_forward(k, h, o).start()
+                ag_far(k, h, o).wait_send()
+                if both_cores(k, h):
+                    ag_near(k, h, o).wait_send()
+                else:
+                    ag_forward(k, h, o).wait_send()
 
     def rs_pair(k, h):
         return remote(
-            part.at[other, :, :, rows(k), cols(h)],
+            part.at[1, :, :, rows(k), cols(h)],
             recv1.at[:, :, rows(k), cols(h)],
             r1_s.at[2 * k + h],
             r1_r.at[2 * k + h],
@@ -107,19 +136,18 @@
         )
 
     def rs_cross(k, h, o):
-        peer = lax.rem(a + o, nt)
         return remote(
-            part.at[b, peer, :, rows(k), cols(h)],
+            part.at[0, o, :, rows(k), cols(h)],
             recv2.at[a, :, rows(k), cols(h)],
             r2_s.at[2 * k + h, o],
             r2_r.at[2 * k + h, a],
-            {"trip": peer},
+            {"trip": trip(o), "sub": other},
         )
 
     def rs_arrive(k, h, o):
-        src = lax.rem(a + o, nt)
+        src = trip(o)
         dst = recv2.at[src, :, rows(k), cols(h)]
-        remote(dst, dst, r2_s.at[2 * k + h, o], r2_r.at[2 * k + h, src], {"trip": src}).wait_recv()
+        remote(dst, dst, r2_s.at[2 * k + h, o], r2_r.at[2 * k + h, src], {"trip": src, "sub": other}).wait_recv()
 
     def z_copy(k, h, o):
         peer = lax.rem(e + o, ne)
@@ -137,14 +165,10 @@
         remote(dst, dst, z_s.at[2 * k + h, o], z_r.at[2 * k + h, src], {"edge": src}).wait_recv()
 
     def lower(k, layer):
-        for h in range(2):
-            f = out[h * half : (h + 1) * half, rows(k), :].reshape(half * CHUNK, de)
-            live = jnp.concatenate([mask[k, h * half * CHUNK : (h + 1) * half * CHUNK, :]] * (ft // 128), axis=1)
-            low = mm3(f, down_h[layer], down_l[layer]) * live
-            gath[me, h * half : (h + 1) * half, rows(k), :] = low.reshape(half, CHUNK, ft)
-            for o in range(1, nt):
-                ag_cross(k, h, o).start()
-            ag_pair(k, h).start()
+        f = out[:, rows(k), :].reshape(eb * CHUNK, de)
+        live = jnp.concatenate([mask[k]] * (ft // 128), axis=1)
+        low = mm3(f, down_h[layer], down_l[layer]) * live
+        gath[me, :, rows(k), :] = low.reshape(eb, CHUNK, ft)
 
     for k in range(nk):
         ids = me * r + k * CHUNK + lax.broadcasted_iota(jnp.int32, (CHUNK, 128), 0)
@@ -162,16 +186,18 @@
         return 0
 
     split_down(0, 0)
-    pl.semaphore_wait(barrier, nt - 1 + 1 + ne - 1)
+    pl.semaphore_wait(barrier, 2 * (nt - 1) + 1 + ne - 1)
     for k in range(nk):
         lower(k, 0)
+        ag_send(k, 0)
+    for k in range(nk):
+        ag_send(k, 1)
     loads[2].wait()
 
     def split_coef(p, _):
         hi, lo = split(coef[tab[o_perm + p]])
-        c3[p, :, 0:blk] = hi
-        c3[p, :, blk : 2 * blk] = lo
-        c3[p, :, 2 * blk : 3 * blk] = hi
+        c2[p, :, 0:blk] = hi
+        c2[p, :, blk : 2 * blk] = lo
         return 0
 
     lax.fori_loop(0, slots, split_coef, 0)
@@ -189,96 +215,111 @@
         return 0
 
     lax.fori_loop(0, layers, split_rest, 0)
-    run[0] = jnp.zeros((blk, ft), F32)
-    for k in range(nk - 2):
-        pass_on(k)
+    for k in range(early):
+        pass_on(k, 0)
 
     def layer_step(layer, _):
-        if nk > 2:
-            pass_on(nk - 2)
-
-        def widen(first):
+        def widen(h, pair):
+            first = 2 * pair * CHUNK
+
             def step(c, _):
                 for rank in range(ranks):
-                    hi, lo = split(gath[rank, c, first : first + 2 * CHUNK, :])
+                    hi, lo = split(gath[rank, c, first : first + 2 * CHUNK, cols(h)])
                     at = rank * r + first
-                    x3[c, at : at + 2 * CHUNK, :] = hi
-                    x3[c, blk + at : blk + at + 2 * CHUNK, :] = hi
-                    x3[c, 2 * blk + at : 2 * blk + at + 2 * CHUNK, :] = lo
+                    x2[h, c, at : at + 2 * CHUNK, 0:wide] = hi
+                    x2[h, c, at : at + 2 * CHUNK, wide : 2 * wide] = lo
                 return 0
 
+            for k in (2 * pair, 2 * pair + 1):
+                ag_arrive(k, h, a * ns + other)
+                for o in range(1, nt):
+                    ag_arrive(k, h, trip(o) * ns + b)
             lax.fori_loop(0, eb, step, 0, unroll=4)
 
+        unroll = 16
+
+        def triplets(h):
+            def step(i, prev):
+                for u in range(unroll):
+                    p = i * unroll + u
+                    keep = tab[o_same + p].astype(F32)
+                    w = x2[h, tab[o_src + p]]
+                    both = dot(c2[p], jnp.concatenate([w, w], axis=0))
+                    prev = prev * keep + (both[:, 0:wide] + both[:, wide : 2 * wide])
+                    run[p] = prev
+                return prev
+
+            lax.fori_loop(0, slots // unroll, step, jnp.zeros((blk, wide), F32))
+
+        def gather_terms(k, h):
+            def collect(t, _):
+                at, has = tab[o_last + t], tab[o_has + t].astype(F32)
+                for o in range(nt):
+                    for i in range(ns):
+                        s = b if (i == 0) == (o == 0) else other
+                        first = pl.multiple_of((trip(o) * ns + s) * r + k * CHUNK, CHUNK)
+                        part[i, o, t, rows(k), cols(h)] = run[at, pl.ds(first, CHUNK), :] * has
+                return 0
+
+            lax.fori_loop(0, eb, collect, 0, unroll=4)
+            rs_pair(k, h).start()
+
+        def cross(k, h):
+            rs_pair(k, h).wait_recv()
+            for o in range(1, nt):
+                part[0, o, :, rows(k), cols(h)] = part[0, o, :, rows(k), cols(h)] + recv1[o, :, rows(k), cols(h)]
+                rs_cross(k, h, o).start()
+            agg[:, rows(k), cols(h)] = part[0, 0, :, rows(k), cols(h)] + recv1[0, :, rows(k), cols(h)]
+
+        def exchange(k, h):
+            total = agg[:, rows(k), cols(h)]
+            for o in range(1, nt):
+                rs_arrive(k, h, o)
+                total = total + recv2[trip(o), :, rows(k), cols(h)]
+            agg[:, rows(k), cols(h)] = total
+            for o in range(1, ne):
+                base = lax.rem(e + o, ne) * cap
+                for s in range(cap):
+                    zs[base + s, rows(k), cols(h)] = agg[tab[o_zsrc + base + s], rows(k), cols(h)]
+                z_copy(k, h, o).start()
+
+        for k in range(early, nk - 1):
+            pass_on(k, 0)
         for pair in range(nk // 2):
             if pair == nk // 2 - 1:
-                for k in range(nk - 1 if nk > 2 else 0, nk):
-                    pass_on(k)
-            for k in (2 * pair, 2 * pair + 1):
-                for h in range(2):
-                    for o in range(nt):
-                        ag_arrive(k, h, lax.rem(a + o, nt) * ns + other)
-            widen(2 * pair * CHUNK)
-        for k in range(nk):
-            for h in range(2):
-                ag_pair(k, h).wait_send()
-                for o in range(1, nt):
-                    ag_cross(k, h, o).wait_send()
-                    ag_forward(k, h, o).wait_send()
-
-        unroll = 16
-
-        def triplets(i, _):
-            for u in range(unroll):
-                p = i * unroll + u
-                keep = tab[o_same + p].astype(F32)
-                run[p + 1] = run[p] * keep + dot(c3[p], x3[tab[o_src + p]])
-            return 0
-
-        lax.fori_loop(0, slots // unroll, triplets, 0)
-
-        def cross(k):
-            for h in range(2):
-                rs_pair(k, h).wait_recv()
-                for o in range(1, nt):
-                    peer = lax.rem(a + o, nt)
-                    part[b, peer, :, rows(k), cols(h)] = (
-                        part[b, peer, :, rows(k), cols(h)] + recv1[peer, :, rows(k), cols(h)]
-                    )
-                    rs_cross(k, h, o).start()
-                agg[:, rows(k), cols(h)] = part[b, a, :, rows(k), cols(h)] + recv1[a, :, rows(k), cols(h)]
-
-        for k in range(nk):
-
-            def collect(t, _):
-                at, has = tab[o_last + t] + 1, tab[o_has + t].astype(F32)
-                for rank in range(ranks):
-                    first = rank * r + k * CHUNK
-                    part[rank % ns, rank // ns, t, rows(k), :] = run[at, first : first + CHUNK, :] * has
-                return 0
-
-            lax.fori_loop(0, eb, collect, 0, unroll=4)
-            for h in range(2):
-                rs_pair(k, h).start()
-            if k > 0:
-                cross(k - 1)
-        cross(nk - 1)
+                pass_on(nk - 1, 0)
+            widen(0, pair)
+        triplets(0)
+        for k in range(nk):
+            pass_on(k, 1)
+        ag_finish(0)
+        for k in range(nk):
+            gather_terms(k, 0)
+        for k in range(2):
+            cross(k, 0)
+        for pair in range(nk // 2):
+            widen(1, pair)
+        triplets(1)
+        ag_finish(1)
+        for k in range(nk):
+            gather_terms(k, 1)
 
         @pl.when(layer > 0)
         def _():
             pl.semaphore_wait(z_free, ne - 1)
 
-        for k in range(nk):
-            for h in range(2):
-                total = agg[:, rows(k), cols(h)]
-                for o in range(1, nt):
-                    rs_arrive(k, h, o)
-                    total = total + recv2[lax.rem(a + o, nt), :, rows(k), cols(h)]
-                agg[:, rows(k), cols(h)] = total
-                for o in range(1, ne):
-                    base = lax.rem(e + o, ne) * cap
-                    for s in range(cap):
-                        zs[base + s, rows(k), cols(h)] = agg[tab[o_zsrc + base + s], rows(k), cols(h)]
-                    z_copy(k, h, o).start()
+        exchange(0, 0)
+        cross(0, 1)
+        cross(1, 1)
+        exchange(1, 0)
+        for k in range(2, nk):
+            cross(k, 0)
+            cross(k, 1)
+        exchange(0, 1)
+        exchange(1, 1)
+        for k in range(2, nk):
+            exchange(k, 0)
+            exchange(k, 1)
         for k in range(nk):
             sides = []
             for h in range(2):
@@ -300,8 +341,10 @@
             @pl.when(layer + 1 < layers)
             def _():
                 lower(k, layer + 1)
-                if k >= 2:
-                    pass_on(k - 2)
+                ag_send(k, 0)
+                ag_send(k, 1)
+                if 2 <= k < early + 2:
+                    pass_on(k - 2, 0)
 
         @pl.when(layer + 1 < layers)
         def _():
@@ -370,9 +413,9 @@
         vm(up_weight.shape, BF16),
         vm(dense_weight.shape, BF16),
         vm(dense_weight.shape, BF16),
-        vm((slots, blk, 3 * blk), BF16),
-        vm((eb, 3 * blk, ft), BF16),
-        vm((slots + 1, blk, ft), F32),
+        vm((slots, blk, 2 * blk), BF16),
+        vm((2, eb, blk, ft), BF16),
+        vm((slots, blk, ft // 2), F32),
         vm((ns, nt, eb, r, ft), F32),
         vm((nt, eb, r, ft), F32),
         vm((nt, eb, r, ft), F32),
@@ -381,6 +424,7 @@
         vm((ranks, eb, r, ft), F32),
         vm((nk, eb * CHUNK, 128), F32),
         dma((6,)),
+        dma((2 * nk, nt)),
         dma((2 * nk, nt)),
         dma((2 * nk,)),
         dma((2 * nk, nt)),

time: 138 us -> 131 us (0.949)
  Pallas kernels: 130 us -> 123 us
    pallas_call x1, Pallas kernels: 130 us -> 123 us  [local(): pl.pallas_call(functools.partial(kernel, dims), out_shape=jax.ShapeDtypeS...]
where the time goes in v1:
time: 131 us
  Pallas kernels  123 us (94%)
  other arithmetic  5.44 us (4%)
  local copies, waits for them, and re-layouts  2.01 us (2%)
    pallas_call x1, Pallas kernels, local(): pl.pallas_call(functools.partial(kernel, dims), out_shape=jax.ShapeDtypeS...  123 us

profile of v1, /device:TPU:0, one launch (start us, length us, event | category | flops | bytes accessed | tf_op | source)
XLA Modules:
  0.0 130.8 jit_solution(1891062255510706881)
XLA Ops:
  0.7 0.7 compare_select_fusion
  1.3 0.7 fusion.6
  2.0 0.1 convert_reduce_fusion.3
  2.1 0.1 fusion.2
  2.2 0.7 slice_bitcast_fusion
  2.9 0.2 fusion
  3.1 0.1 select_reduce_fusion
  3.3 0.7 and_select_fusion.2
  4.0 0.2 convert_reduce_fusion.1
  4.2 0.2 convert_reduce_fusion.2
  4.4 0.1 select_reduce_fusion.3
  4.5 1.3 %concatenate.3.tab = s32[288]{0:T(512)} concatenate(s32[64]{0:T(128)S(1)} %get-tuple-element.7, s32[64]{0:T(128)S(1)} %get-tuple-element.6, s32[64]{0:T(128)S(1)} %get-tuple-element.5, s32[16]{0:T(128)S(1)} %get-tuple-element.14, s32[16]{0:T(128)S(1)} %convert_element_type.30, s32[32]{0:T(128)S(1)} %select_reduce_fusion.3, s32[16]{0:T(128)S(1)} %get-tuple-element.12, s32[16]{0:T(128)} %param.10), dimensions={0} | concatenate | bytes 2304 | tf_op jit(solution)/shard_map/concatenate | solution.py:400
  5.8 122.7 %shard_map.91 = f32[16,32,512]{2,1,0:T(8,128)} custom-call(s32[288]{0:T(512)} %concatenate.3.tab, f32[16,32,512]{2,1,0:T(8,128)} %feat_hbm.1, f32[64,128,128]{2,1,0:T(8,128)} %bitcast.7, f32[3,512,256]{2,1,0:T(8,128)} %down_hbm.1, f32[3,256,512]{2,1,0:T(8,128)} %up_hbm.1, f32[3,512,512]{2,1,0:T(8,128)} %dense_hbm.1), custom_call_target="tpu_custom_call" | custom-call | tf_op jit(solution)/shard_map/pallas_call | solution.py:441
  128.5 2.3 %broadcast_multiply_fusion = f32[16,32,512]{2,1,0:T(8,128)} fusion(f32[16,32,512]{2,1,0:T(8,128)} %shard_map.91), kind=kLoop, calls=%fused_computation | loop fusion | flops 262144 | bytes 2097152 | tf_op jit(solution)/shard_map/mul | solution.py:449
  (4 shorter events, 0.0 us)

commit v2 on v1

--- a/solution.py
+++ b/solution.py
@@ -30,18 +30,54 @@
     return both[:rows] + both[rows:] + dot(hi, w_lo)
 
 
-def kernel(dims, tab, feat_hbm, coef_hbm, down_hbm, up_hbm, dense_hbm, out, *scratch):
+def build_tables(dims, e, live_slots, pattern, rev, table):
+    nt, ns, ne, eb, r, cap, slots, layers, blk, ft, de = dims
+
+    def down_rows(cond, value):
+        return jnp.sum(jnp.where(cond, value, 0), axis=0, keepdims=True)
+
+    def along(cond, value):
+        return jnp.sum(jnp.where(cond, value, 0), axis=1, keepdims=True)
+
+    def put(row, value, size):
+        table[row : row + 1, 0 : value.shape[1]] = jnp.minimum(jnp.maximum(value, 0), size - 1)
+
+    def grids(n):
+        return (lax.broadcasted_iota(jnp.int32, (n, n), d) for d in (0, 1))
+
+    i, j = grids(slots)
+    key_j = jnp.where(j < live_slots[...], pattern[0:1, :], eb)
+    key, source = along(i == j, key_j), along(i == j, pattern[1:2, :])
+    rank = along((key_j < key) | ((key_j == key) & (j < i)), 1)
+    again = jnp.minimum(along((key_j == key) & (j < i), 1), 1)
+    hot = rank == j
+    put(0, down_rows(hot, i), slots)
+    put(1, down_rows(hot, source), eb)
+    put(2, down_rows(hot, again), 2)
+    put(3, down_rows(key <= j, 1) - 1, slots)
+    put(4, down_rows(key == j, 1), 2)
+
+    i, j = grids(ne * eb)
+
+    def owner(x):
+        return sum((x >= d * eb).astype(jnp.int32) for d in range(1, ne))
+
+    to_j = rev[...]
+    to = along(i == j, to_j)
+    of_i, of_j, of_to = owner(i), owner(j), owner(to)
+    slot = along((j < i) & (of_j == of_i) & (owner(to_j) == of_to), 1)
+    base = e * eb
+    put(5, down_rows((of_i == e) & (of_to * cap + slot == j), i - base), eb)
+    put(6, down_rows(to == j + base, of_i * cap + slot), ne * cap)
+
+
+def kernel(dims, counts, live_slots, pattern, rev, feat_hbm, coef_hbm, down_hbm, up_hbm, dense_hbm, out, *scratch):
     nt, ns, ne, eb, r, cap, slots, layers, blk, ft, de = dims
     nk, ranks, wide = r // CHUNK, nt * ns, ft // 2
     early = nk - 2 if nk > 2 else 0
     zr, scratch = scratch[: 2 * nk], scratch[2 * nk :]
-    (coef, down, up, dense, down_h, down_l, up_h, up_l, dense_h, dense_l, c2, x2, run, part, recv1, recv2, agg, zs, gath, mask,
-     in_sem, agx_s, agy_s, agp_s, agf_s, ag_r, r1_s, r1_r, r2_s, r2_r, z_s, z_r, z_free) = scratch
-    o_perm, o_src, o_same = 0, slots, 2 * slots
-    o_last, o_has = 3 * slots, 3 * slots + eb
-    o_zsrc = o_has + eb
-    o_zpos = o_zsrc + ne * cap
-    o_count = o_zpos + eb
+    (coef, down, up, dense, down_h, down_l, up_h, up_l, dense_h, dense_l, c2, x2, run, part, recv1, recv2, agg, zs, gath, mask, table, tab,
+     tab_sem, in_sem, agx_s, agy_s, agp_s, agf_s, ag_r, r1_s, r1_r, r2_s, r2_r, z_s, z_r, z_free) = scratch
     a, b, e = lax.axis_index("trip"), lax.axis_index("sub"), lax.axis_index("edge")
     other = lax.rem(b + 1, ns)
     me = a * ns + b
@@ -173,7 +209,7 @@
     for k in range(nk):
         ids = me * r + k * CHUNK + lax.broadcasted_iota(jnp.int32, (CHUNK, 128), 0)
         for c in range(eb):
-            mask[k, c * CHUNK : (c + 1) * CHUNK, :] = jnp.where(ids < tab[o_count + c], 1.0, 0.0).astype(F32)
+            mask[k, c * CHUNK : (c + 1) * CHUNK, :] = jnp.where(ids < counts[c], 1.0, 0.0).astype(F32)
     loads[5].wait()
     loads[0].wait()
     for i in (2, 3, 4, 1):
@@ -192,10 +228,13 @@
         ag_send(k, 0)
     for k in range(nk):
         ag_send(k, 1)
+    build_tables(dims, e, live_slots, pattern, rev, table)
+    to_scalar = pltpu.make_async_copy(table, tab, tab_sem)
+    to_scalar.start()
     loads[2].wait()
 
     def split_coef(p, _):
-        hi, lo = split(coef[tab[o_perm + p]])
+        hi, lo = split(coef[p])
         c2[p, :, 0:blk] = hi
         c2[p, :, blk : 2 * blk] = lo
         return 0
@@ -215,6 +254,7 @@
         return 0
 
     lax.fori_loop(0, layers, split_rest, 0)
+    to_scalar.wait()
     for k in range(early):
         pass_on(k, 0)
 
@@ -236,15 +276,15 @@
                     ag_arrive(k, h, trip(o) * ns + b)
             lax.fori_loop(0, eb, step, 0, unroll=4)
 
-        unroll = 16
+        unroll = slots
 
         def triplets(h):
             def step(i, prev):
                 for u in range(unroll):
                     p = i * unroll + u
-                    keep = tab[o_same + p].astype(F32)
-                    w = x2[h, tab[o_src + p]]
-                    both = dot(c2[p], jnp.concatenate([w, w], axis=0))
+                    keep = tab[2, p].astype(F32)
+                    w = x2[h, tab[1, p]]
+                    both = dot(c2[tab[0, p]], jnp.concatenate([w, w], axis=0))
                     prev = prev * keep + (both[:, 0:wide] + both[:, wide : 2 * wide])
                     run[p] = prev
                 return prev
@@ -253,7 +293,7 @@
 
         def gather_terms(k, h):
             def collect(t, _):
-                at, has = tab[o_last + t], tab[o_has + t].astype(F32)
+                at, has = tab[3, t], tab[4, t].astype(F32)
                 for o in range(nt):
                     for i in range(ns):
                         s = b if (i == 0) == (o == 0) else other
@@ -280,7 +320,7 @@
             for o in range(1, ne):
                 base = lax.rem(e + o, ne) * cap
                 for s in range(cap):
-                    zs[base + s, rows(k), cols(h)] = agg[tab[o_zsrc + base + s], rows(k), cols(h)]
+                    zs[base + s, rows(k), cols(h)] = agg[tab[5, base + s], rows(k), cols(h)]
                 z_copy(k, h, o).start()
 
         for k in range(early, nk - 1):
@@ -327,7 +367,7 @@
                     z_arrive(k, h, o)
                 sides.append(
                     jnp.concatenate(
-                        [agg[c, rows(k), cols(h)] + zr[2 * k + h][tab[o_zpos + c]] for c in range(eb)], axis=0
+                        [agg[c, rows(k), cols(h)] + zr[2 * k + h][tab[6, c]] for c in range(eb)], axis=0
                     )
                 )
             both = jnp.concatenate(sides, axis=1)
@@ -369,36 +409,7 @@
     layers, _, ft = down_weight.shape
     _, _, slots, blk, _ = coef.shape
     nk, ranks = r // CHUNK, nt * ns
-    edge_rank = lax.axis_index("edge")
     cap = 2 * ((eb // 2 + ne // 2 - 1) // (ne // 2))
-    i32 = jnp.int32
-    ids = jnp.arange(slots, dtype=i32)
-    key = jnp.where(ids < trip_count[0, 0], patterns[0, 0, :, 0], eb)
-    before = (key[None, :] < key[:, None]) | ((key[None, :] == key[:, None]) & (ids[None, :] < ids[:, None]))
-    rank = jnp.sum(before.astype(i32), axis=1)
-    hot = (rank[None, :] == ids[:, None]).astype(i32)
-    perm = jnp.sum(hot * ids[None, :], axis=1)
-    source = jnp.sum(hot * patterns[0, 0, :, 1][None, :], axis=1)
-    first = jnp.sum((key[None, :] < key[:, None]).astype(i32), axis=1)
-    same = jnp.sum(hot * (first < rank).astype(i32)[None, :], axis=1)
-    cl = jnp.arange(eb, dtype=i32)
-    upto = jnp.sum((key[None, :] <= cl[:, None]).astype(i32), axis=1)
-    has = jnp.any(key[None, :] == cl[:, None], axis=1).astype(i32)
-    last = jnp.maximum(upto - 1, 0)
-    mine = lax.dynamic_slice_in_dim(reverse, edge_rank * eb, eb)
-    dev = mine // eb
-    send_slot = jnp.sum(((dev[:, None] == dev[None, :]) & (cl[None, :] < cl[:, None])).astype(i32), axis=1)
-    zslots = jnp.arange(ne * cap, dtype=i32)
-    zsrc = jnp.sum(jnp.where(zslots[:, None] == (dev * cap + send_slot)[None, :], cl[None, :], 0), axis=1)
-    all_ids = jnp.arange(reverse.shape[0], dtype=i32)
-    match = (
-        (all_ids[None, :] // eb == dev[:, None])
-        & (all_ids[None, :] < mine[:, None])
-        & (reverse[None, :] // eb == edge_rank)
-    )
-    zpos = dev * cap + jnp.sum(match.astype(i32), axis=1)
-    tab = jnp.concatenate([perm, source, same, last, has, zsrc, zpos, edge_counts]).astype(i32)
-
     dims = (nt, ns, ne, eb, r, cap, slots, layers, blk, ft, de)
     vm = pltpu.VMEM
     dma = pltpu.SemaphoreType.DMA
@@ -423,6 +434,9 @@
         vm((ne * cap, r, ft), F32),
         vm((ranks, eb, r, ft), F32),
         vm((nk, eb * CHUNK, 128), F32),
+        vm((8, max(128, ne * eb, slots)), jnp.int32),
+        pltpu.SMEM((8, max(128, ne * eb, slots)), jnp.int32),
+        dma,
         dma((6,)),
         dma((2 * nk, nt)),
         dma((2 * nk, nt)),
@@ -441,11 +455,11 @@
     unscaled = pl.pallas_call(
         functools.partial(kernel, dims),
         out_shape=jax.ShapeDtypeStruct(edge_feat.shape, F32),
-        in_specs=[pl.BlockSpec(memory_space=pltpu.SMEM)] + [anywhere] * 5,
+        in_specs=[pl.BlockSpec(memory_space=pltpu.SMEM)] + [pl.BlockSpec(memory_space=pltpu.VMEM)] * 3 + [anywhere] * 5,
         out_specs=pl.BlockSpec(memory_space=pltpu.VMEM),
         scratch_shapes=scratch,
         compiler_params=pltpu.CompilerParams(collective_id=0, has_side_effects=True, vmem_limit_bytes=64 * 1024 * 1024 - 65536),
-    )(tab, edge_feat, coef[0, 0], down_weight, up_weight, dense_weight)
+    )(edge_counts, trip_count, patterns[0, 0].T, reverse[None, :], edge_feat, coef[0, 0], down_weight, up_weight, dense_weight)
     return unscaled * INV_TWO
 
 

time: 131 us -> 125 us (0.954)
  other arithmetic: 5.44 us -> 2.32 us
  local copies, waits for them, and re-layouts: 2.01 us -> 0 us
    select_n x3 -> x0, other arithmetic: 1.43 us -> none  [the longest x1 0.74 us: local(): dev = mine // eb]
    concatenate x1 -> x0, local copies, waits for them, and re-layouts: 1.32 us -> none  [local(): jnp.concatenate([perm, source, same, last, has, zsrc, zpos, edge_counts])]
where the time goes in v2:
time: 125 us
  Pallas kernels  122 us (98%)
  other arithmetic  2.32 us (2%)
    pallas_call x1, Pallas kernels, local(): pl.pallas_call(functools.partial(kernel, dims), out_shape=jax.ShapeDtypeS...  122 us

profile of v2, /device:TPU:0, one launch (start us, length us, event | category | flops | bytes accessed | tf_op | source)
XLA Modules:
  0.0 124.9 jit_solution(4116020888406711049)
XLA Ops:
  0.7 121.9 %shard_map.91 = f32[16,32,512]{2,1,0:T(8,128)} custom-call(s32[16]{0:T(128)} %counts.1, s32[1,1]{1,0:T(1,128)S(6)} %copy.10.live_slots, s32[2,64]{1,0:T(2,128)} %bitcast.6, s32[1,64]{1,0:T(1,128)} %bitcast.7, f32[16,32,512]{2,1,0:T(8,128)} %feat_hbm.1, f32[64,128,128]{2,1,0:T(8,128)} %bitcast.5, f32[3,512,256]{2,1,0:T(8,128)} %down_hbm.1, ...), custom_call_target="tpu_custom_call" | custom-call | tf_op jit(solution)/shard_map/pallas_call | solution.py:455
  122.6 2.3 %broadcast_multiply_fusion = f32[16,32,512]{2,1,0:T(8,128)} fusion(f32[16,32,512]{2,1,0:T(8,128)} %shard_map.91), kind=kLoop, calls=%fused_computation | loop fusion | flops 262144 | bytes 2097152 | tf_op jit(solution)/shard_map/mul | solution.py:463

commit v3 on v2

--- a/solution.py
+++ b/solution.py
@@ -71,13 +71,13 @@
     put(6, down_rows(to == j + base, of_i * cap + slot), ne * cap)
 
 
-def kernel(dims, counts, live_slots, pattern, rev, feat_hbm, coef_hbm, down_hbm, up_hbm, dense_hbm, out, *scratch):
+def kernel(dims, counts, live_slots, pattern, rev, feat_hbm, coef_hbm, down_hbm, up_hbm, dense_hbm, out_hbm, *scratch):
     nt, ns, ne, eb, r, cap, slots, layers, blk, ft, de = dims
     nk, ranks, wide = r // CHUNK, nt * ns, ft // 2
     early = nk - 2 if nk > 2 else 0
     zr, scratch = scratch[: 2 * nk], scratch[2 * nk :]
-    (coef, down, up, dense, down_h, down_l, up_h, up_l, dense_h, dense_l, c2, x2, run, part, recv1, recv2, agg, zs, gath, mask, table, tab,
-     tab_sem, in_sem, agx_s, agy_s, agp_s, agf_s, ag_r, r1_s, r1_r, r2_s, r2_r, z_s, z_r, z_free) = scratch
+    (out, coef, down, up, dense, down_h, down_l, up_h, up_l, dense_h, dense_l, c2, x2, run, part, recv1, recv2, agg, zs, gath, mask, table, tab,
+     tab_sem, out_sem, in_sem, agx_s, agy_s, agp_s, agf_s, ag_r, r1_s, r1_r, r2_s, r2_r, z_s, z_r, z_free) = scratch
     a, b, e = lax.axis_index("trip"), lax.axis_index("sub"), lax.axis_index("edge")
     other = lax.rem(b + 1, ns)
     me = a * ns + b
@@ -85,10 +85,12 @@
     rest = pl.ds(1, layers - 1)
     loads = [
         pltpu.make_async_copy(s, d, in_sem.at[i])
-        for i, (s, d) in enumerate(((feat_hbm, out), (down_hbm.at[rest], down.at[rest]), (coef_hbm, coef), (up_hbm, up), (dense_hbm, dense), (down_hbm.at[0], down.at[0])))
+        for i, (s, d) in enumerate([(feat_hbm.at[:, pl.ds(k * CHUNK, CHUNK), :], out.at[:, pl.ds(k * CHUNK, CHUNK), :]) for k in range(nk)] + [(down_hbm.at[rest], down.at[rest]), (coef_hbm, coef), (up_hbm, up), (dense_hbm, dense), (down_hbm.at[0], down.at[0])])
     ]
-    loads[5].start()
-    loads[0].start()
+    l_down, l_coef, l_up, l_dense, l_first = range(nk, nk + 5)
+    loads[l_first].start()
+    for k in range(nk):
+        loads[k].start()
 
     barrier = pltpu.get_barrier_semaphore()
     for o in range(1, nt):
@@ -108,6 +110,9 @@
         return pltpu.make_async_remote_copy(
             src_ref=src, dst_ref=dst, send_sem=send, recv_sem=recv, device_id=where, device_id_type=MESH
         )
+
+    def finished(k):
+        return pltpu.make_async_copy(out.at[:, rows(k), :], out_hbm.at[:, rows(k), :], out_sem.at[k])
 
     def trip(o):
         return lax.rem(a + o, nt)
@@ -210,9 +215,8 @@
         ids = me * r + k * CHUNK + lax.broadcasted_iota(jnp.int32, (CHUNK, 128), 0)
         for c in range(eb):
             mask[k, c * CHUNK : (c + 1) * CHUNK, :] = jnp.where(ids < counts[c], 1.0, 0.0).astype(F32)
-    loads[5].wait()
-    loads[0].wait()
-    for i in (2, 3, 4, 1):
+    loads[l_first].wait()
+    for i in (l_coef, l_up, l_dense, l_down):
         loads[i].start()
 
     def split_down(i, _):
@@ -222,16 +226,18 @@
         return 0
 
     split_down(0, 0)
-    pl.semaphore_wait(barrier, 2 * (nt - 1) + 1 + ne - 1)
     for k in range(nk):
+        loads[k].wait()
         lower(k, 0)
+        if k == 0:
+            pl.semaphore_wait(barrier, 2 * (nt - 1) + 1 + ne - 1)
         ag_send(k, 0)
     for k in range(nk):
         ag_send(k, 1)
     build_tables(dims, e, live_slots, pattern, rev, table)
     to_scalar = pltpu.make_async_copy(table, tab, tab_sem)
     to_scalar.start()
-    loads[2].wait()
+    loads[l_coef].wait()
 
     def split_coef(p, _):
         hi, lo = split(coef[p])
@@ -240,7 +246,7 @@
         return 0
 
     lax.fori_loop(0, slots, split_coef, 0)
-    for i in (3, 4, 1):
+    for i in (l_up, l_dense, l_down):
         loads[i].wait()
     lax.fori_loop(1, layers, split_down, 0)
 
@@ -274,7 +280,7 @@
                 ag_arrive(k, h, a * ns + other)
                 for o in range(1, nt):
                     ag_arrive(k, h, trip(o) * ns + b)
-            lax.fori_loop(0, eb, step, 0, unroll=4)
+            lax.fori_loop(0, eb, step, 0, unroll=eb)
 
         unroll = slots
 
@@ -301,7 +307,7 @@
                         part[i, o, t, rows(k), cols(h)] = run[at, pl.ds(first, CHUNK), :] * has
                 return 0
 
-            lax.fori_loop(0, eb, collect, 0, unroll=4)
+            lax.fori_loop(0, eb, collect, 0, unroll=eb)
             rs_pair(k, h).start()
 
         def cross(k, h):
@@ -330,28 +336,32 @@
                 pass_on(nk - 1, 0)
             widen(0, pair)
         triplets(0)
+        gather_terms(0, 0)
+        gather_terms(1, 0)
         for k in range(nk):
             pass_on(k, 1)
-        ag_finish(0)
-        for k in range(nk):
+        cross(0, 0)
+        cross(1, 0)
+        for k in range(2, nk):
             gather_terms(k, 0)
-        for k in range(2):
-            cross(k, 0)
         for pair in range(nk // 2):
             widen(1, pair)
         triplets(1)
-        ag_finish(1)
-        for k in range(nk):
-            gather_terms(k, 1)
 
         @pl.when(layer > 0)
         def _():
             pl.semaphore_wait(z_free, ne - 1)
 
         exchange(0, 0)
+        ag_finish(0)
+        ag_finish(1)
+        gather_terms(0, 1)
+        gather_terms(1, 1)
+        exchange(1, 0)
+        for k in range(2, nk):
+            gather_terms(k, 1)
         cross(0, 1)
         cross(1, 1)
-        exchange(1, 0)
         for k in range(2, nk):
             cross(k, 0)
             cross(k, 1)
@@ -378,6 +388,10 @@
             new = (mixed + v / (1.0 + jnp.exp(-v))) * jnp.where(layer + 1 < layers, INV_TWO, 1.0)
             out[:, rows(k), :] = new.reshape(eb, CHUNK, de)
 
+            @pl.when(layer + 1 == layers)
+            def _():
+                finished(k).start()
+
             @pl.when(layer + 1 < layers)
             def _():
                 lower(k, layer + 1)
@@ -401,6 +415,8 @@
         return 0
 
     lax.fori_loop(0, layers, layer_step, 0)
+    for k in range(nk):
+        finished(k).wait()
 
 
 def local(edge_feat, edge_counts, reverse, patterns, trip_count, coef, down_weight, up_weight, dense_weight):
@@ -414,6 +430,7 @@
     vm = pltpu.VMEM
     dma = pltpu.SemaphoreType.DMA
     scratch = [vm((ne * cap, CHUNK, ft // 2), F32) for _ in range(2 * nk)] + [
+        vm(edge_feat.shape, F32),
         vm((slots, blk, blk), F32),
         vm(down_weight.shape, F32),
         vm(up_weight.shape, F32),
@@ -437,7 +454,8 @@
         vm((8, max(128, ne * eb, slots)), jnp.int32),
         pltpu.SMEM((8, max(128, ne * eb, slots)), jnp.int32),
         dma,
-        dma((6,)),
+        dma((nk,)),
+        dma((nk + 5,)),
         dma((2 * nk, nt)),
         dma((2 * nk, nt)),
         dma((2 * nk,)),
@@ -456,7 +474,7 @@
         functools.partial(kernel, dims),
         out_shape=jax.ShapeDtypeStruct(edge_feat.shape, F32),
         in_specs=[pl.BlockSpec(memory_space=pltpu.SMEM)] + [pl.BlockSpec(memory_space=pltpu.VMEM)] * 3 + [anywhere] * 5,
-        out_specs=pl.BlockSpec(memory_space=pltpu.VMEM),
+        out_specs=anywhere,
         scratch_shapes=scratch,
         compiler_params=pltpu.CompilerParams(collective_id=0, has_side_effects=True, vmem_limit_bytes=64 * 1024 * 1024 - 65536),
     )(edge_counts, trip_count, patterns[0, 0].T, reverse[None, :], edge_feat, coef[0, 0], down_weight, up_weight, dense_weight)

time: 125 us -> 123 us (0.984)
  Pallas kernels: 122 us -> 119 us
    pallas_call x1, Pallas kernels: 122 us -> 119 us  [local(): pl.pallas_call(functools.partial(kernel, dims), out_shape=jax.ShapeDtypeS...]
where the time goes in v3:
time: 123 us; the launch traced here: 122 us
  Pallas kernels  119 us (97%)
  other arithmetic  2.32 us (2%)
    pallas_call x1, Pallas kernels, local(): pl.pallas_call(functools.partial(kernel, dims), out_shape=jax.ShapeDtypeS...  119 us

profile of v3, /device:TPU:0, one launch (start us, length us, event | category | flops | bytes accessed | tf_op | source)
XLA Modules:
  0.0 122.4 jit_solution(14337910293985895483)
XLA Ops:
  0.7 119.4 %shard_map.91 = f32[16,32,512]{2,1,0:T(8,128)} custom-call(s32[16]{0:T(128)} %counts.1, s32[1,1]{1,0:T(1,128)S(6)} %copy.10.live_slots, s32[2,64]{1,0:T(2,128)} %bitcast.6, s32[1,64]{1,0:T(1,128)} %bitcast.7, f32[16,32,512]{2,1,0:T(8,128)} %feat_hbm.1, f32[64,128,128]{2,1,0:T(8,128)} %bitcast.5, f32[3,512,256]{2,1,0:T(8,128)} %down_hbm.1, ...), custom_call_target="tpu_custom_call" | custom-call | tf_op jit(solution)/shard_map/pallas_call | solution.py:473
  120.1 2.3 %broadcast_multiply_fusion = f32[16,32,512]{2,1,0:T(8,128)} fusion(f32[16,32,512]{2,1,0:T(8,128)} %shard_map.91), kind=kLoop, calls=%fused_computation | loop fusion | flops 262144 | bytes 2097152 | tf_op jit(solution)/shard_map/mul | solution.py:481

commit v4 on v3

--- a/solution.py
+++ b/solution.py
@@ -77,7 +77,7 @@
     early = nk - 2 if nk > 2 else 0
     zr, scratch = scratch[: 2 * nk], scratch[2 * nk :]
     (out, coef, down, up, dense, down_h, down_l, up_h, up_l, dense_h, dense_l, c2, x2, run, part, recv1, recv2, agg, zs, gath, mask, table, tab,
-     tab_sem, out_sem, in_sem, agx_s, agy_s, agp_s, agf_s, ag_r, r1_s, r1_r, r2_s, r2_r, z_s, z_r, z_free) = scratch
+     tab_sem, out_sem, in_sem, agx_s, agp_s, agf_s, ag_r, r1_s, r1_r, r2_s, r2_r, z_s, z_r, z_free) = scratch
     a, b, e = lax.axis_index("trip"), lax.axis_index("sub"), lax.axis_index("edge")
     other = lax.rem(b + 1, ns)
     me = a * ns + b
@@ -94,8 +94,7 @@
 
     barrier = pltpu.get_barrier_semaphore()
     for o in range(1, nt):
-        for s in (b, other):
-            pl.semaphore_signal(barrier, inc=1, device_id={"trip": lax.rem(a + o, nt), "sub": s}, device_id_type=MESH)
+        pl.semaphore_signal(barrier, inc=1, device_id={"trip": lax.rem(a + o, nt)}, device_id_type=MESH)
     pl.semaphore_signal(barrier, inc=1, device_id={"sub": other}, device_id_type=MESH)
     for o in range(1, ne):
         pl.semaphore_signal(barrier, inc=1, device_id={"edge": lax.rem(e + o, ne)}, device_id_type=MESH)
@@ -117,26 +116,19 @@
     def trip(o):
         return lax.rem(a + o, nt)
 
-    def both_cores(k, h):
-        return False
-
     def gather_piece(rank, k, h):
         return gath.at[rank, :, rows(k), cols(h)]
 
     def ag_far(k, h, o):
         g = gather_piece(me, k, h)
-        return remote(g, g, agx_s.at[2 * k + h, o], ag_r.at[2 * k + h, me], {"trip": trip(o), "sub": other})
-
-    def ag_near(k, h, o):
-        g = gather_piece(me, k, h)
-        return remote(g, g, agy_s.at[2 * k + h, o], ag_r.at[2 * k + h, me], {"trip": trip(o), "sub": b})
+        return remote(g, g, agx_s.at[2 * k + h, o], ag_r.at[2 * k + h, me], {"trip": trip(o)})
 
     def ag_pair(k, h):
         g = gather_piece(me, k, h)
         return remote(g, g, agp_s.at[2 * k + h], ag_r.at[2 * k + h, me], {"sub": other})
 
     def ag_forward(k, h, o):
-        rank = trip(o) * ns + other
+        rank = trip(o) * ns + b
         g = gather_piece(rank, k, h)
         return remote(g, g, agf_s.at[2 * k + h, o], ag_r.at[2 * k + h, rank], {"sub": other})
 
@@ -147,25 +139,19 @@
     def ag_send(k, h):
         for o in range(1, nt):
             ag_far(k, h, o).start()
-            if both_cores(k, h):
-                ag_near(k, h, o).start()
         ag_pair(k, h).start()
 
     def pass_on(k, h):
         for o in range(1, nt):
-            ag_arrive(k, h, trip(o) * ns + other)
-            if not both_cores(k, h):
-                ag_forward(k, h, o).start()
+            ag_arrive(k, h, trip(o) * ns + b)
+            ag_forward(k, h, o).start()
 
     def ag_finish(h):
         for k in range(nk):
             ag_pair(k, h).wait_send()
             for o in range(1, nt):
                 ag_far(k, h, o).wait_send()
-                if both_cores(k, h):
-                    ag_near(k, h, o).wait_send()
-                else:
-                    ag_forward(k, h, o).wait_send()
+                ag_forward(k, h, o).wait_send()
 
     def rs_pair(k, h):
         return remote(
@@ -182,13 +168,13 @@
             recv2.at[a, :, rows(k), cols(h)],
             r2_s.at[2 * k + h, o],
             r2_r.at[2 * k + h, a],
-            {"trip": trip(o), "sub": other},
+            {"trip": trip(o)},
         )
 
     def rs_arrive(k, h, o):
         src = trip(o)
         dst = recv2.at[src, :, rows(k), cols(h)]
-        remote(dst, dst, r2_s.at[2 * k + h, o], r2_r.at[2 * k + h, src], {"trip": src, "sub": other}).wait_recv()
+        remote(dst, dst, r2_s.at[2 * k + h, o], r2_r.at[2 * k + h, src], {"trip": src}).wait_recv()
 
     def z_copy(k, h, o):
         peer = lax.rem(e + o, ne)
@@ -230,7 +216,7 @@
         loads[k].wait()
         lower(k, 0)
         if k == 0:
-            pl.semaphore_wait(barrier, 2 * (nt - 1) + 1 + ne - 1)
+            pl.semaphore_wait(barrier, nt - 1 + 1 + ne - 1)
         ag_send(k, 0)
     for k in range(nk):
         ag_send(k, 1)
@@ -279,7 +265,7 @@
             for k in (2 * pair, 2 * pair + 1):
                 ag_arrive(k, h, a * ns + other)
                 for o in range(1, nt):
-                    ag_arrive(k, h, trip(o) * ns + b)
+                    ag_arrive(k, h, trip(o) * ns + other)
             lax.fori_loop(0, eb, step, 0, unroll=eb)
 
         unroll = slots
@@ -302,7 +288,7 @@
                 at, has = tab[3, t], tab[4, t].astype(F32)
                 for o in range(nt):
                     for i in range(ns):
-                        s = b if (i == 0) == (o == 0) else other
+                        s = b if i == 0 else other
                         first = pl.multiple_of((trip(o) * ns + s) * r + k * CHUNK, CHUNK)
                         part[i, o, t, rows(k), cols(h)] = run[at, pl.ds(first, CHUNK), :] * has
                 return 0
@@ -457,7 +443,6 @@
         dma((nk,)),
         dma((nk + 5,)),
         dma((2 * nk, nt)),
-        dma((2 * nk, nt)),
         dma((2 * nk,)),
         dma((2 * nk, nt)),
         dma((2 * nk, ranks)),

time: 123 us -> 121 us (0.984)
    pallas_call x1, Pallas kernels: 119 us -> 118 us  [local(): pl.pallas_call(functools.partial(kernel, dims), out_shape=jax.ShapeDtypeS...]
where the time goes in v4:
time: 121 us
  Pallas kernels  118 us (98%)
  other arithmetic  2.32 us (2%)
    pallas_call x1, Pallas kernels, local(): pl.pallas_call(functools.partial(kernel, dims), out_shape=jax.ShapeDtypeS...  118 us

profile of v4, /device:TPU:0, one launch (start us, length us, event | category | flops | bytes accessed | tf_op | source)
XLA Modules:
  0.0 120.6 jit_solution(8467119367689817228)
XLA Ops:
  0.7 117.6 %shard_map.91 = f32[16,32,512]{2,1,0:T(8,128)} custom-call(s32[16]{0:T(128)} %counts.1, s32[1,1]{1,0:T(1,128)S(6)} %copy.10.live_slots, s32[2,64]{1,0:T(2,128)} %bitcast.6, s32[1,64]{1,0:T(1,128)} %bitcast.7, f32[16,32,512]{2,1,0:T(8,128)} %feat_hbm.1, f32[64,128,128]{2,1,0:T(8,128)} %bitcast.5, f32[3,512,256]{2,1,0:T(8,128)} %down_hbm.1, ...), custom_call_target="tpu_custom_call" | custom-call | tf_op jit(solution)/shard_map/pallas_call | solution.py:458
  118.3 2.3 %broadcast_multiply_fusion = f32[16,32,512]{2,1,0:T(8,128)} fusion(f32[16,32,512]{2,1,0:T(8,128)} %shard_map.91), kind=kLoop, calls=%fused_computation | loop fusion | flops 262144 | bytes 2097152 | tf_op jit(solution)/shard_map/mul | solution.py:466

commit v5 on v4

--- a/solution.py
+++ b/solution.py
@@ -317,6 +317,11 @@
 
         for k in range(early, nk - 1):
             pass_on(k, 0)
+        @pl.when(layer > 0)
+        def _():
+            for k in range(nk - 1):
+                pass_on(k, 1)
+
         for pair in range(nk // 2):
             if pair == nk // 2 - 1:
                 pass_on(nk - 1, 0)
@@ -324,8 +329,13 @@
         triplets(0)
         gather_terms(0, 0)
         gather_terms(1, 0)
-        for k in range(nk):
-            pass_on(k, 1)
+
+        @pl.when(layer == 0)
+        def _():
+            for k in range(nk - 1):
+                pass_on(k, 1)
+
+        pass_on(nk - 1, 1)
         cross(0, 0)
         cross(1, 0)
         for k in range(2, nk):

time: 121 us -> 121 us (level)
  no operation moved by 1% of the time
where the time goes in v5:
time: 121 us
  Pallas kernels  118 us (98%)
  other arithmetic  2.32 us (2%)
    pallas_call x1, Pallas kernels, local(): pl.pallas_call(functools.partial(kernel, dims), out_shape=jax.ShapeDtypeS...  118 us

profile of v5, /device:TPU:0, one launch (start us, length us, event | category | flops | bytes accessed | tf_op | source)
XLA Modules:
  0.0 120.6 jit_solution(337428029407320900)
XLA Ops:
  0.7 117.7 %shard_map.91 = f32[16,32,512]{2,1,0:T(8,128)} custom-call(s32[16]{0:T(128)} %counts.1, s32[1,1]{1,0:T(1,128)S(6)} %copy.10.live_slots, s32[2,64]{1,0:T(2,128)} %bitcast.6, s32[1,64]{1,0:T(1,128)} %bitcast.7, f32[16,32,512]{2,1,0:T(8,128)} %feat_hbm.1, f32[64,128,128]{2,1,0:T(8,128)} %bitcast.5, f32[3,512,256]{2,1,0:T(8,128)} %down_hbm.1, ...), custom_call_target="tpu_custom_call" | custom-call | tf_op jit(solution)/shard_map/pallas_call | solution.py:468
  118.3 2.3 %broadcast_multiply_fusion = f32[16,32,512]{2,1,0:T(8,128)} fusion(f32[16,32,512]{2,1,0:T(8,128)} %shard_map.91), kind=kLoop, calls=%fused_computation | loop fusion | flops 262144 | bytes 2097152 | tf_op jit(solution)/shard_map/mul | solution.py:476
